TPU v7x, 512 devices: a whole 4x8x8 slice. The times are simulated.
512 devices in a mesh: rows: 64 (over y, z), grp: 8 (over x, core).
Axes of the slice: x: 4, y: 8, z: 8, core: 2. Of those that a mesh axis runs over, the one named last changes fastest.
Arguments:
- basis: float32 [64, 2097152], P(None, ('rows', 'grp'))
- values: float32 [64], replicated, may hold values from 0.5 to 20
- archive: bfloat16 [64, 2097152], P('grp', 'rows')
- window_ids: int32 [32], replicated, may hold values from 0 to 63, as said below
Outputs:
- filtered: float32 [96, 2097152], P(None, ('rows', 'grp'))
- projector: float32 [96, 96], replicated
- novelty: float32 [32], replicated
Inputs may be any that keep to these rules, and one draw needn't show every extreme that they name: `window_ids`: distinct; 0 and 63 are always among them.
All inputs are finite; a program needn't handle non-finite values.
Results may differ from a plain program's by a relative error of at most 0.0003.
Values may be sent and summed in bfloat16 or wider, within the bound.
No kernel may reach another device: no remote copies, remote signals or barrier semaphores. Data moves between devices by JAX's collectives and lax.ppermute only.
A program may use at most 64 MiB of HBM per device.

v0:
```python
import math
import jax
import jax.numpy as jnp
from jax import lax
from jax.sharding import PartitionSpec as P

NEWTON = 10
HIGH = lax.Precision.HIGHEST


def spectral(core):
    width = core.shape[0]
    identity = jnp.eye(width, dtype=jnp.float32)
    square = jnp.dot(core, core.T, precision=HIGH)
    total = jnp.trace(square)
    shifted = (square - total / width * identity) / total
    for iteration in range(NEWTON):
        cubed = jnp.dot(jnp.dot(shifted, shifted, precision=HIGH), shifted, precision=HIGH)
        shifted = 1.5 * shifted - 0.5 * cubed
    return 0.5 * (identity + shifted)


def inverse_lower(gram):
    factor = jnp.linalg.cholesky(gram)
    identity = jnp.eye(gram.shape[0], dtype=jnp.float32)
    return (factor, jax.scipy.linalg.solve_triangular(factor, identity, lower=True))


def per_device(basis, values, archive, window_ids):
    mode_count = basis.shape[0]
    window_count = window_ids.shape[0]
    local_rows = basis.shape[1]
    total_rows = local_rows * lax.axis_size("rows") * lax.axis_size("grp")
    everything = lax.all_to_all(archive, "grp", split_axis=1, concat_axis=0, tiled=True)
    picker = (
        window_ids[:, None] == jnp.arange(everything.shape[0], dtype=jnp.int32)[None, :]
    ).astype(jnp.bfloat16)
    gathered = jnp.dot(picker, everything, preferred_element_type=jnp.float32)
    columns = gathered * (1.0 / math.sqrt(total_rows))
    proj_part = jnp.einsum("kr,pr->kp", basis, columns, precision=HIGH)
    energy_part = jnp.sum(columns * columns, axis=1)
    projection, energy = lax.psum((proj_part, energy_part), ("rows", "grp"))
    resid = columns - jnp.einsum("kp,kr->pr", projection, basis, precision=HIGH)
    gram_one = lax.psum(jnp.einsum("pr,qr->pq", resid, resid, precision=HIGH), ("rows", "grp"))
    factor_one, inverse_one = inverse_lower(gram_one)
    first = jnp.dot(inverse_one, resid, precision=HIGH)
    gram_two = lax.psum(jnp.einsum("pr,qr->pq", first, first, precision=HIGH), ("rows", "grp"))
    factor_two, inverse_two = inverse_lower(gram_two)
    ortho = jnp.dot(inverse_two, first, precision=HIGH)
    upper = jnp.dot(factor_two.T, factor_one.T, precision=HIGH)
    top_rows = jnp.concatenate([jnp.diag(values), projection], axis=1)
    low_rows = jnp.concatenate([jnp.zeros((window_count, mode_count), jnp.float32), upper], axis=1)
    core = jnp.concatenate([top_rows, low_rows], axis=0)
    projector = spectral(core)
    weights = jnp.dot(core.T, projector, precision=HIGH)
    stacked = jnp.concatenate([basis, ortho], axis=0)
    filtered = jnp.dot(weights, stacked, precision=HIGH) * math.sqrt(total_rows)
    novelty = jnp.diagonal(gram_one) / energy
    return (filtered, projector, novelty)


def solution(mesh):
    placed = (P(None, ("rows", "grp")), P(), P("grp", "rows"), P())
    return jax.shard_map(
        per_device,
        mesh=mesh,
        in_specs=placed,
        out_specs=(P(None, ("rows", "grp")), P(), P()),
        check_vma=False,
    )
```

profile of v0, /device:TPU:26, one launch (start us, length us, event | category | flops | bytes accessed | tf_op | source)
XLA Modules:
  0.0 340.1 jit_solution(17657873917726056590)
XLA Ops:
  0.6 5.0 %all-to-all-start = ((bf16[8,8,4096]{2,0,1:T(8,128)(2,1)}), bf16[8,8,4096]{2,0,1:T(8,128)(2,1)S(1)}, u32[]{:S(2)}, u32[]{:S(2)}) async-start(bf16[8,8,4096]{2,0,1:T(8,128)(2,1)} %bitcast.81), calls=%async_computation | async-start | bytes 1048576 | tf_op jit(solution)/shard_map/all_to_all | solution.py:34
  5.6 0.7 fusion.16
  6.4 8.1 %all-to-all-done = bf16[8,8,4096]{2,0,1:T(8,128)(2,1)S(1)} async-done(((bf16[8,8,4096]{2,0,1:T(8,128)(2,1)}), bf16[8,8,4096]{2,0,1:T(8,128)(2,1)S(1)}, u32[]{:S(2)}, u32[]{:S(2)}) %all-to-all-start) | async-done | bytes 524320 | tf_op jit(solution)/shard_map/all_to_all | solution.py:34
  14.5 1.0 multiply_reduce_fusion
  15.5 1.0 convolution_bitcast_fusion
  16.5 104.3 %psum.28 = f32[64,32]{0,1:T(8,128)S(1)} all-reduce(f32[64,32]{0,1:T(8,128)S(1)} %convolution_bitcast_fusion), channel_id=1, replica_groups=mesh['rows'=64,'grp'=8] {'rows','grp'}, use_global_device_ids=true, to_apply=%region_0.0 | all-reduce | flops 2048 | bytes 16384 | tf_op jit(solution)/shard_map/psum | solution.py:42
  120.8 0.6 convolution_subtract_fusion
  122.0 94.5 %psum.29 = f32[32,32]{0,1:T(8,128)S(1)} all-reduce(f32[32,32]{0,1:T(8,128)S(1)} %fusion.51), channel_id=1, replica_groups=mesh['rows'=64,'grp'=8] {'rows','grp'}, use_global_device_ids=true, to_apply=%region_1.0 | all-reduce | flops 1024 | bytes 8192 | tf_op jit(solution)/shard_map/psum | solution.py:44
  216.6 2.9 cholesky.44
  219.6 0.6 compare_reduce_fusion.1
  220.2 0.7 fusion.29
  220.9 2.4 custom-call.8
  224.7 95.4 %all-reduce.1 = (f32[32,32]{0,1:T(8,128)S(1)}, f32[32]{0:T(128)S(1)}) all-reduce(f32[32,32]{0,1:T(8,128)S(1)} %fusion.53, f32[32]{0:T(128)S(1)} %get-tuple-element.7), channel_id=1, replica_groups=mesh['rows'=64,'grp'=8] {'rows','grp'}, use_global_device_ids=true, to_apply=%region_4.0 | all-reduce | flops 1056 | bytes 8448 | tf_op jit(solution)/shard_map/psum | solution.py:47
  320.2 2.9 cholesky.55
  323.2 0.6 compare_reduce_fusion
  323.8 1.5 fusion.30
  325.3 0.7 select_bitcast_fusion
  326.0 0.7 gather_fusion
  326.7 2.4 custom-call.9
  329.4 0.6 fusion.63
  330.0 0.9 select_reduce_fusion
  331.5 0.8 fusion.34
  332.4 0.8 fusion.14
  337.5 2.6 convolution_multiply_fusion
  (37 shorter events, 6.6 us)
Async XLA Ops:
  0.6 14.9 %copy-start = (f32[64,4096]{1,0:T(8,128)S(1)}, f32[64,4096]{1,0:T(8,128)}, u32[]{:S(2)}) copy-start(f32[64,4096]{1,0:T(8,128)} %param.7) | copy-start | bytes 3145732
  0.6 13.8 %all-to-all-start = ((bf16[8,8,4096]{2,0,1:T(8,128)(2,1)}), bf16[8,8,4096]{2,0,1:T(8,128)(2,1)S(1)}, u32[]{:S(2)}, u32[]{:S(2)}) async-start(bf16[8,8,4096]{2,0,1:T(8,128)(2,1)} %bitcast.81), calls=%async_computation | async-start | bytes 1048576 | tf_op jit(solution)/shard_map/all_to_all | solution.py:34
  336.6 3.5 %copy-start.1 = (f32[96,96]{1,0:T(8,128)}, f32[96,96]{1,0:T(8,128)S(1)}, u32[]{:S(2)}) copy-start(f32[96,96]{1,0:T(8,128)S(1)} %fusion.5) | copy-start | bytes 110596
where the time goes:
time: 341 us; the launch traced here: 340 us
  blocking collectives  294 us (86%)
  matrix products  15.7 us (5%)
  other arithmetic  14.7 us (4%)
  waiting for transfers between devices  8.12 us (2%)
  starting transfers between devices  4.97 us (1%)
    psum x1, blocking collectives, per_device(): projection, energy = lax.psum((proj_part, energy_part), ('rows', 'grp'))  104 us
    psum x1, blocking collectives, per_device(): lax.psum(jnp.einsum('pr,qr->pq', first, first, precision=HIGH), ('rows',...  95.4 us
    psum x1, blocking collectives, per_device(): lax.psum(jnp.einsum('pr,qr->pq', resid, resid, precision=HIGH), ('rows',...  94.5 us
    all_to_all x1, waiting for transfers between devices, per_device(): lax.all_to_all(archive, 'grp', split_axis=1, concat_axis=0, tiled=True)  8.12 us
    another operation x6, other arithmetic, inverse_lower(): factor = jnp.linalg.cholesky(gram)  7.19 us
  transfers between devices with their start and end apart: 1, of which 1 were waited for; matrix products, arithmetic and copies ran while one was open for 0% of the time, Pallas kernels for 0%

commit v1 on v0

--- a/solution.py
+++ b/solution.py
@@ -39,7 +39,7 @@
     columns = gathered * (1.0 / math.sqrt(total_rows))
     proj_part = jnp.einsum("kr,pr->kp", basis, columns, precision=HIGH)
     energy_part = jnp.sum(columns * columns, axis=1)
-    projection, energy = lax.psum((proj_part, energy_part), ("rows", "grp"))
+    projection, energy = lax.psum(lax.psum((proj_part, energy_part), "rows"), "grp")
     resid = columns - jnp.einsum("kp,kr->pr", projection, basis, precision=HIGH)
     gram_one = lax.psum(jnp.einsum("pr,qr->pq", resid, resid, precision=HIGH), ("rows", "grp"))
     factor_one, inverse_one = inverse_lower(gram_one)

time: 341 us -> 545 us (1.60)
  the two profiles are of different devices: /device:TPU:26 before, /device:TPU:1 now
where the time goes in v1:
time: 545 us
  blocking collectives  493 us (90%)
  matrix products  15.7 us (3%)
  other arithmetic  14.7 us (3%)
  starting transfers between devices  10.4 us (2%)
  waiting for transfers between devices  8.64 us (2%)
    psum x1, blocking collectives, per_device(): lax.psum((proj_part, energy_part), 'rows')  227 us
    psum x1, blocking collectives, per_device(): lax.psum(jnp.einsum('pr,qr->pq', first, first, precision=HIGH), ('rows',...  95.5 us
    psum x1, blocking collectives, per_device(): lax.psum(jnp.einsum('pr,qr->pq', resid, resid, precision=HIGH), ('rows',...  95.1 us
    psum x1, blocking collectives, per_device(): lax.psum(lax.psum((proj_part, energy_part), 'rows'), 'grp')  75.8 us
  transfers between devices with their start and end apart: 1, of which 1 were waited for; matrix products, arithmetic and copies ran while one was open for 0% of the time, Pallas kernels for 0%

profile of v1, /device:TPU:1, one launch (start us, length us, event | category | flops | bytes accessed | tf_op | source)
XLA Modules:
  0.0 544.8 jit_solution(2936949378837340428)
XLA Ops:
  0.6 10.4 %all-to-all-start = ((bf16[8,8,4096]{2,0,1:T(8,128)(2,1)}), bf16[8,8,4096]{2,0,1:T(8,128)(2,1)S(1)}, u32[]{:S(2)}, u32[]{:S(2)}) async-start(bf16[8,8,4096]{2,0,1:T(8,128)(2,1)} %bitcast.81), calls=%async_computation | async-start | bytes 1048576 | tf_op jit(solution)/shard_map/all_to_all | solution.py:34
  11.0 0.7 fusion.16
  11.8 8.6 %all-to-all-done = bf16[8,8,4096]{2,0,1:T(8,128)(2,1)S(1)} async-done(((bf16[8,8,4096]{2,0,1:T(8,128)(2,1)}), bf16[8,8,4096]{2,0,1:T(8,128)(2,1)S(1)}, u32[]{:S(2)}, u32[]{:S(2)}) %all-to-all-start) | async-done | bytes 524320 | tf_op jit(solution)/shard_map/all_to_all | solution.py:34
  20.4 1.0 multiply_reduce_fusion
  21.4 1.0 convolution_bitcast_fusion
  22.4 226.6 %all-reduce.1 = (f32[64,32]{0,1:T(8,128)S(1)}, f32[32]{0:T(128)S(1)}) all-reduce(f32[64,32]{0,1:T(8,128)S(1)} %convolution_bitcast_fusion, f32[32]{0:T(128)S(1)} %get-tuple-element.9), channel_id=1, replica_groups=mesh['rows'=64,'grp'=8] {'rows'}, use_global_device_ids=true, to_apply=%region_0.0 | all-reduce | flops 2080 | bytes 16640 | tf_op jit(solution)/shard_map/psum | solution.py:42
  249.0 75.8 %all-reduce.2 = (f32[64,32]{0,1:T(8,128)S(1)}, f32[32]{0:T(128)S(1)}) all-reduce(f32[64,32]{0,1:T(8,128)S(1)} %get-tuple-element.5, f32[32]{0:T(128)S(1)} %get-tuple-element.6), channel_id=1, replica_groups=mesh['rows'=64,'grp'=8] {'grp'}, use_global_device_ids=true, to_apply=%region_1.0 | all-reduce | flops 2080 | bytes 16640 | tf_op jit(solution)/shard_map/psum | solution.py:42
  324.8 0.6 convolution_subtract_fusion
  326.1 95.1 %psum.44 = f32[32,32]{0,1:T(8,128)S(1)} all-reduce(f32[32,32]{0,1:T(8,128)S(1)} %fusion.51), channel_id=1, replica_groups=mesh['rows'=64,'grp'=8] {'rows','grp'}, use_global_device_ids=true, to_apply=%region_2.0 | all-reduce | flops 1024 | bytes 8192 | tf_op jit(solution)/shard_map/psum | solution.py:44
  421.3 2.9 cholesky.44
  424.3 0.6 compare_reduce_fusion.1
  424.9 0.7 fusion.29
  425.6 2.4 custom-call.8
  429.4 95.5 %psum.45 = f32[32,32]{0,1:T(8,128)S(1)} all-reduce(f32[32,32]{0,1:T(8,128)S(1)} %fusion.53), channel_id=1, replica_groups=mesh['rows'=64,'grp'=8] {'rows','grp'}, use_global_device_ids=true, to_apply=%region_5.8 | all-reduce | flops 1024 | bytes 8192 | tf_op jit(solution)/shard_map/psum | solution.py:47
  525.0 2.9 cholesky.55
  527.9 0.6 compare_reduce_fusion
  528.6 1.5 fusion.30
  530.1 0.7 select_bitcast_fusion
  530.7 0.7 gather_fusion
  531.5 2.4 custom-call.9
  534.7 0.9 select_reduce_fusion
  536.3 0.8 fusion.34
  537.1 0.8 fusion.14
  542.2 2.6 convolution_multiply_fusion
  (38 shorter events, 7.2 us)
Async XLA Ops:
  0.6 20.8 %copy-start = (f32[64,4096]{1,0:T(8,128)S(1)}, f32[64,4096]{1,0:T(8,128)}, u32[]{:S(2)}) copy-start(f32[64,4096]{1,0:T(8,128)} %param.7) | copy-start | bytes 3145732
  0.6 19.8 %all-to-all-start = ((bf16[8,8,4096]{2,0,1:T(8,128)(2,1)}), bf16[8,8,4096]{2,0,1:T(8,128)(2,1)S(1)}, u32[]{:S(2)}, u32[]{:S(2)}) async-start(bf16[8,8,4096]{2,0,1:T(8,128)(2,1)} %bitcast.81), calls=%async_computation | async-start | bytes 1048576 | tf_op jit(solution)/shard_map/all_to_all | solution.py:34
  541.3 3.5 copy-start.1
